TPU v7x, 32 devices: a whole 2x2x4 slice. The times are simulated.
32 devices in a mesh: col: 4 (over x, core), slab: 8 (over z, y).
Axes of the slice: x: 2, y: 2, z: 4, core: 2. Of those that a mesh axis runs over, the one named last changes fastest.
Arguments:
- labels: int32 [32, 64, 128], P('col', 'slab'), may hold values from 0 to 2
- table: float32 [3], replicated, may hold values from 0.3 to 3
- factor: float32 [32, 64, 128], P('col', 'slab'), may hold values from 0.5 to 2
- chi: float32 [3, 32, 64, 128], P(None, 'col', 'slab'), may hold values from -2.5 to 2.5
- weights: float32 [3, 3], replicated, may hold values from -3.5 to 3.5
Outputs:
- adjoint: float32 [3, 32, 64, 128], P(None, 'col', 'slab')
- gradient: float32 [32, 64, 128], P('col', 'slab')
All inputs are finite; a program needn't handle non-finite values.
Results may differ from a plain program's by a relative error of at most 0.0001.
Values sent between devices are 32-bit elements; how exact they have to be, the bound alone decides.
No kernel may reach another device: no remote copies, remote signals or barrier semaphores. Data moves between devices by JAX's collectives and lax.ppermute only.
A program may use at most 64 MiB of HBM per device.

v0:
```python
import jax
import jax.numpy as jnp
from jax import lax
from jax.sharding import PartitionSpec as P

ITERS = 3
mass_shift = 0.01


def extended(block, sides, width):
    for axis, dim in sides:
        count = lax.axis_size(axis)
        forward = [(i, i + 1) for i in range(count - 1)]
        forward.append((count - 1, 0))
        backward = [(target, source) for source, target in forward]
        low = lax.ppermute(
            lax.slice_in_dim(block, block.shape[dim] - width, None, axis=dim), axis, forward
        )
        high = lax.ppermute(lax.slice_in_dim(block, 0, width, axis=dim), axis, backward)
        block = jnp.concatenate([low, block, high], axis=dim)
    return block


def neighbour_pair(padded, field, spatial):
    if spatial == 0:
        return (padded[..., :-1, 1:-1, :], padded[..., 1:, 1:-1, :])
    if spatial == 1:
        return (padded[..., 1:-1, :-1, :], padded[..., 1:-1, 1:, :])
    return (field, jnp.roll(field, -1, axis=-1))


def split_faces(full, spatial):
    if spatial == 0:
        return (full[..., 1:, :, :], full[..., :-1, :, :])
    if spatial == 1:
        return (full[..., :, 1:, :], full[..., :, :-1, :])
    return (full, jnp.roll(full, 1, axis=-1))


def neighbours(padded, centre, spatial):
    if spatial == 0:
        return (padded[:, :-2, 1:-1, :], padded[:, 2:, 1:-1, :])
    if spatial == 1:
        return (padded[:, 1:-1, :-2, :], padded[:, 1:-1, 2:, :])
    return (jnp.roll(centre, 1, axis=-1), jnp.roll(centre, -1, axis=-1))


def widen(values):
    return values[:, None, None, None]


def apply_operator(padded, centre, cond_full):
    result = mass_shift * centre
    for d in range(3):
        c_now, c_prev = split_faces(cond_full[d], d)
        before, after = neighbours(padded, centre, d)
        result = result + c_now * (centre - after) + c_prev * (centre - before)
    return result


def squares(residual):
    return lax.psum(jnp.sum(residual * residual, axis=(1, 2, 3)), ("col", "slab"))


def shards(labels, table, factor, chi, weights):
    conduct = jnp.where(labels == 0, table[0], jnp.where(labels == 1, table[1], table[2])) * factor
    stacked = jnp.concatenate([chi, conduct[None]], axis=0)
    padded = extended(stacked, (("col", 1), ("slab", 2)), 1)
    chi_pad = padded[:3]
    cond_pad = padded[3]
    cond_full, strain_full, kpairs = ([], [], [])
    for d in range(3):
        here, after = neighbour_pair(cond_pad, conduct, d)
        cond_full.append(2.0 * here * after / (here + after))
        kpairs.append((here, after))
        c_here, c_after = neighbour_pair(chi_pad, chi, d)
        strain_full.append(
            jnp.stack([(1.0 if j == d else 0.0) + (c_after[j] - c_here[j]) for j in range(3)])
        )
    drive = jnp.zeros_like(chi)
    for d in range(3):
        flux_now, flux_prev = split_faces(cond_full[d] * strain_full[d], d)
        drive = drive + (flux_prev - flux_now)
    source = jnp.stack(
        [
            weights[i, 0] * drive[0] + weights[i, 1] * drive[1] + weights[i, 2] * drive[2]
            for i in range(3)
        ]
    )
    adjoint = jnp.zeros_like(source)
    residual = source
    direction = source
    norm_now = squares(residual)
    for step in range(ITERS):
        dir_pad = extended(direction, (("col", 1), ("slab", 2)), 1)
        image = apply_operator(dir_pad, direction, cond_full)
        curve = lax.psum(jnp.sum(direction * image, axis=(1, 2, 3)), ("col", "slab"))
        alpha = norm_now / curve
        adjoint = adjoint + widen(alpha) * direction
        residual = residual - widen(alpha) * image
        norm_next = squares(residual)
        direction = residual + widen(norm_next / norm_now) * direction
        norm_now = norm_next
    lam_pad = extended(adjoint, (("col", 1), ("slab", 2)), 1)
    gradient = jnp.zeros_like(conduct)
    for d in range(3):
        lam_here, lam_after = neighbour_pair(lam_pad, adjoint, d)
        lam_diff = lam_after - lam_here
        local = strain_full[d]
        energy = jnp.zeros_like(local[0])
        for i in range(3):
            for j in range(3):
                energy = energy + weights[i, j] * local[i] * local[j]
        h_term = energy - (lam_diff[0] * local[0] + lam_diff[1] * local[1] + lam_diff[2] * local[2])
        here, after = kpairs[d]
        square_sum = (here + after) ** 2
        part_here = 2.0 * after * after / square_sum
        part_after = 2.0 * here * here / square_sum
        term_now, unused_prev = split_faces(h_term * part_here, d)
        unused_now, term_prev = split_faces(h_term * part_after, d)
        gradient = gradient + term_now + term_prev
    return (adjoint, gradient)


def solution(mesh):
    in_specs = (
        P("col", "slab", None),
        P(),
        P("col", "slab", None),
        P(None, "col", "slab", None),
        P(),
    )
    out_specs = (P(None, "col", "slab", None), P("col", "slab", None))
    return jax.shard_map(shards, mesh=mesh, in_specs=in_specs, out_specs=out_specs, check_vma=False)
```

profile of v0, /device:TPU:0, one launch (start us, length us, event | category | flops | bytes accessed | tf_op | source)
XLA Modules:
  0.0 283.4 jit_solution(14369096348308002320)
XLA Ops:
  0.6 1.4 fusion.147
  2.0 2.6 select_multiply_fusion
  5.1 2.0 collective-permute-start.1
  9.1 5.4 %collective-permute-start.3 = (f32[4,10,1,128]{3,2,1,0:T(1,128)S(1)}, f32[4,10,1,128]{3,2,1,0:T(1,128)S(1)}, u32[]{:S(2)}, u32[]{:S(2)}) collective-permute-start(f32[4,10,1,128]{3,2,1,0:T(1,128)S(1)} %get-tuple-element.19), channel_id=1, source_target_pairs={{1,0},{2,1},{3,2},{4,3},{5,4},{6,5},{7,6},{0,7},{9,8},{10,9},{11,1... | collective-permute-start | bytes 61448 | tf_op jit(solution)/shard_map/ppermute | solution.py:19
  14.5 1.5 collective-permute-done.3
  15.9 5.1 %collective-permute-done.2 = f32[4,10,1,128]{3,2,1,0:T(1,128)S(1)} collective-permute-done((f32[4,10,1,128]{3,2,1,0:T(1,128)S(1)}, f32[4,10,1,128]{3,2,1,0:T(1,128)S(1)}, u32[]{:S(2)}, u32[]{:S(2)}) %collective-permute-start.2) | collective-permute-done | bytes 20512 | tf_op jit(solution)/shard_map/ppermute | solution.py:16
  21.3 5.6 %multiply_add_fusion.5 = (f32[1,8,8,128]{3,2,1,0:T(8,128)S(1)}, f32[1,8,8,128]{3,2,1,0:T(8,128)S(1)}, f32[1,8,8,128]{3,2,1,0:T(8,128)S(1)}) fusion(f32[3,8,8,128]{3,2,1,0:T(8,128)S(1)} %fusion.46, f32[]{:T(128)} %bitcast.7, f32[]{:T(128)} %bitcast.6, f32[]{:T(128)} %bitcast, f32[]{:T(128)} %bitcast.10, f32[]{:T(128)} %bitcast.9, f32[]{:T(128)} %bitcast.8, ...), kind=kLoop, calls=%fused_computation.280 | loop fusion | flops 122880 | bytes 196644 | tf_op jit(solution)/shard_map/add | solution.py:86
  27.3 1.7 collective-permute-start.4
  29.1 1.3 collective-permute-done.5
  30.5 2.0 collective-permute-start.7
  32.5 1.7 collective-permute-done.6
  34.2 2.8 collective-permute-done.7
  37.2 36.9 %all-reduce = (f32[3]{0:T(128)S(1)}, f32[3]{0:T(128)S(1)}) all-reduce(f32[3]{0:T(128)S(1)} %get-tuple-element.3, f32[3]{0:T(128)S(1)} %get-tuple-element.2), channel_id=1, replica_groups=mesh['col'=4,'slab'=8] {'col','slab'}, use_global_device_ids=true, to_apply=%region_1.2 | all-reduce | flops 6 | bytes 48 | tf_op jit(solution)/shard_map/psum | solution.py:62
  74.3 42.2 %psum.44 = f32[3]{0:T(128)S(1)} all-reduce(f32[3]{0:T(128)S(1)} %get-tuple-element.10), channel_id=1, replica_groups=mesh['col'=4,'slab'=8] {'col','slab'}, use_global_device_ids=true, to_apply=%region_5.6 | all-reduce | flops 3 | bytes 24 | tf_op jit(solution)/shard_map/psum | solution.py:62
  116.7 1.7 collective-permute-start.8
  118.5 1.3 collective-permute-done.9
  119.9 3.3 %collective-permute-start.10 = (f32[3,10,1,128]{3,2,1,0:T(1,128)S(1)}, f32[3,10,1,128]{3,2,1,0:T(1,128)S(1)}, u32[]{:S(2)}, u32[]{:S(2)}) collective-permute-start(f32[3,10,1,128]{3,2,1,0:T(1,128)S(1)} %get-tuple-element.27), channel_id=1, source_target_pairs={{1,0},{2,1},{3,2},{4,3},{5,4},{6,5},{7,6},{0,7},{9,8},{10,9},{11,1... | collective-permute-start | bytes 46088 | tf_op jit(solution)/shard_map/ppermute | solution.py:19
  123.3 1.3 collective-permute-done.10
  124.6 5.0 %collective-permute-done.11 = f32[3,10,1,128]{3,2,1,0:T(1,128)S(1)} collective-permute-done((f32[3,10,1,128]{3,2,1,0:T(1,128)S(1)}, f32[3,10,1,128]{3,2,1,0:T(1,128)S(1)}, u32[]{:S(2)}, u32[]{:S(2)}) %collective-permute-start.11) | collective-permute-done | bytes 15392 | tf_op jit(solution)/shard_map/ppermute | solution.py:16
  129.8 36.8 %psum.45 = f32[3]{0:T(128)S(1)} all-reduce(f32[3]{0:T(128)S(1)} %get-tuple-element.8), channel_id=1, replica_groups=mesh['col'=4,'slab'=8] {'col','slab'}, use_global_device_ids=true, to_apply=%region_7.8 | all-reduce | flops 3 | bytes 24 | tf_op jit(solution)/shard_map/psum | solution.py:97
  166.9 41.4 %psum.46 = f32[3]{0:T(128)S(1)} all-reduce(f32[3]{0:T(128)S(1)} %multiply_reduce_fusion), channel_id=1, replica_groups=mesh['col'=4,'slab'=8] {'col','slab'}, use_global_device_ids=true, to_apply=%region_9.10 | all-reduce | flops 3 | bytes 24 | tf_op jit(solution)/shard_map/psum | solution.py:62
  208.5 1.7 collective-permute-start.12
  210.3 1.3 collective-permute-done.13
  211.7 3.3 %collective-permute-start.14 = (f32[3,10,1,128]{3,2,1,0:T(1,128)S(1)}, f32[3,10,1,128]{3,2,1,0:T(1,128)S(1)}, u32[]{:S(2)}, u32[]{:S(2)}) collective-permute-start(f32[3,10,1,128]{3,2,1,0:T(1,128)S(1)} %get-tuple-element.25), channel_id=1, source_target_pairs={{1,0},{2,1},{3,2},{4,3},{5,4},{6,5},{7,6},{0,7},{9,8},{10,9},{11,1... | collective-permute-start | bytes 46088 | tf_op jit(solution)/shard_map/ppermute | solution.py:19
  215.1 1.3 collective-permute-done.14
  216.4 5.0 %collective-permute-done.15 = f32[3,10,1,128]{3,2,1,0:T(1,128)S(1)} collective-permute-done((f32[3,10,1,128]{3,2,1,0:T(1,128)S(1)}, f32[3,10,1,128]{3,2,1,0:T(1,128)S(1)}, u32[]{:S(2)}, u32[]{:S(2)}) %collective-permute-start.15) | collective-permute-done | bytes 15392 | tf_op jit(solution)/shard_map/ppermute | solution.py:16
  221.6 36.8 %psum.47 = f32[3]{0:T(128)S(1)} all-reduce(f32[3]{0:T(128)S(1)} %fusion.7), channel_id=1, replica_groups=mesh['col'=4,'slab'=8] {'col','slab'}, use_global_device_ids=true, to_apply=%region_11.12 | all-reduce | flops 3 | bytes 24 | tf_op jit(solution)/shard_map/psum | solution.py:97
  258.8 1.7 collective-permute-start.16
  260.6 5.7 %fusion.94 = (f32[8,8,128]{2,1,0:T(8,128)S(1)}, f32[8,8,128]{2,1,0:T(8,128)S(1)}) fusion(f32[8,8,128]{2,1,0:T(8,128)S(1)} %select_multiply_fusion, f32[8,8,1]{2,1,0:T(8,128)S(1)} %bitcast.219, f32[8,8,127]{2,1,0:T(8,128)S(1)} %slice.582, f32[3,8,8,128]{3,2,1,0:T(8,128)S(1)} %maximum_subtract_fusion.8, f32[]{:T(128)} %bitcast.13, f32[]{:T(128)} %bitcast.12, ...), kind=kLoop, calls=%fused_computation.222 | loop fusion | flops 319488 | bytes 327716 | tf_op jit(solution)/shard_map/mul | solution.py:120
  266.4 4.0 %collective-permute-start.18 = (f32[3,10,1,128]{3,2,1,0:T(1,128)S(1)}, f32[3,10,1,128]{3,2,1,0:T(1,128)S(1)}, u32[]{:S(2)}, u32[]{:S(2)}) collective-permute-start(f32[3,10,1,128]{3,2,1,0:T(1,128)S(1)} %get-tuple-element.23), channel_id=1, source_target_pairs={{1,0},{2,1},{3,2},{4,3},{5,4},{6,5},{7,6},{0,7},{9,8},{10,9},{11,1... | collective-permute-start | bytes 46088 | tf_op jit(solution)/shard_map/ppermute | solution.py:19
  270.5 5.7 %fusion.81 = f32[9,8,128]{2,1,0:T(8,128)S(1)} fusion(f32[3,9,8,128]{3,2,1,0:T(8,128)S(1)} %maximum_subtract_fusion, f32[1,9,8,128]{3,2,1,0:T(8,128)S(1)} %get-tuple-element.18, f32[1,9,8,128]{3,2,1,0:T(8,128)S(1)} %get-tuple-element.17, f32[1,9,8,128]{3,2,1,0:T(8,128)S(1)} %get-tuple-element.16, f32[]{:T(128)} %bitcast.13, f32[]{:T(128)} %bitcast.12, ...), kind=kLoop, calls=%fused_computation.190 | loop fusion | flops 294912 | bytes 258084 | tf_op jit(solution)/shard_map/sub | solution.py:114
  276.9 5.7 %fusion.62 = f32[8,9,128]{2,1,0:T(8,128)S(1)} fusion(f32[3,8,9,128]{3,2,1,0:T(8,128)S(1)} %fusion, f32[1,8,9,128]{3,2,1,0:T(8,128)S(1)} %fusion.68, f32[1,8,9,128]{3,2,1,0:T(8,128)S(1)} %fusion.69, f32[1,8,9,128]{3,2,1,0:T(8,128)S(1)} %maximum_subtract_fusion.10, f32[]{:T(128)} %bitcast.13, f32[]{:T(128)} %bitcast.12, f32[]{:T(128)} %bitcast.11, ...), kind=kLoop, calls=%fused_computation.137 | loop fusion | flops 294912 | bytes 258084 | tf_op jit(solution)/shard_map/sub | solution.py:114
  (81 shorter events, 6.9 us)
Async XLA Ops:
  0.6 4.0 %copy-start = (f32[3,8,8,128]{3,2,1,0:T(8,128)S(1)}, f32[3,8,8,128]{3,2,1,0:T(8,128)}, u32[]{:S(2)}) copy-start(f32[3,8,8,128]{3,2,1,0:T(8,128)} %param.8) | copy-start | bytes 294916
  4.6 4.4 %collective-permute-start = (f32[4,1,8,128]{3,2,1,0:T(8,128)S(1)}, f32[4,1,8,128]{3,2,1,0:T(8,128)S(1)}, u32[]{:S(2)}, u32[]{:S(2)}) collective-permute-start(f32[4,1,8,128]{3,2,1,0:T(8,128)S(1)} %get-tuple-element.21), channel_id=1, source_target_pairs={{0,8},{8,16},{16,24},{24,0},{1,9},{9,17},{17,25},{25,1},{2,10},{10... | collective-permute-start | bytes 49160 | tf_op jit(solution)/shard_map/ppermute | solution.py:16
  5.1 3.9 %collective-permute-start.1 = (f32[4,1,8,128]{3,2,1,0:T(8,128)S(1)}, f32[4,1,8,128]{3,2,1,0:T(8,128)S(1)}, u32[]{:S(2)}, u32[]{:S(2)}) collective-permute-start(f32[4,1,8,128]{3,2,1,0:T(8,128)S(1)} %get-tuple-element.22), channel_id=1, source_target_pairs={{8,0},{16,8},{24,16},{0,24},{9,1},{17,9},{25,17},{1,25},{10,2},{18... | collective-permute-start | bytes 49160 | tf_op jit(solution)/shard_map/ppermute | solution.py:19
  7.5 0.7 copy-start.2
  9.1 6.8 %collective-permute-start.3 = (f32[4,10,1,128]{3,2,1,0:T(1,128)S(1)}, f32[4,10,1,128]{3,2,1,0:T(1,128)S(1)}, u32[]{:S(2)}, u32[]{:S(2)}) collective-permute-start(f32[4,10,1,128]{3,2,1,0:T(1,128)S(1)} %get-tuple-element.19), channel_id=1, source_target_pairs={{1,0},{2,1},{3,2},{4,3},{5,4},{6,5},{7,6},{0,7},{9,8},{10,9},{11,1... | collective-permute-start | bytes 61448 | tf_op jit(solution)/shard_map/ppermute | solution.py:19
  14.5 6.5 %collective-permute-start.2 = (f32[4,10,1,128]{3,2,1,0:T(1,128)S(1)}, f32[4,10,1,128]{3,2,1,0:T(1,128)S(1)}, u32[]{:S(2)}, u32[]{:S(2)}) collective-permute-start(f32[4,10,1,128]{3,2,1,0:T(1,128)S(1)} %get-tuple-element.20), channel_id=1, source_target_pairs={{0,1},{1,2},{2,3},{3,4},{4,5},{5,6},{6,7},{7,0},{8,9},{9,10},{10,1... | collective-permute-start | bytes 61448 | tf_op jit(solution)/shard_map/ppermute | solution.py:16
  27.2 3.2 %collective-permute-start.5 = (f32[3,1,8,128]{3,2,1,0:T(8,128)S(1)}, f32[3,1,8,128]{3,2,1,0:T(8,128)S(1)}, u32[]{:S(2)}, u32[]{:S(2)}) collective-permute-start(f32[3,1,8,128]{3,2,1,0:T(8,128)S(1)} %get-tuple-element.45), channel_id=1, source_target_pairs={{0,8},{8,16},{16,24},{24,0},{1,9},{9,17},{17,25},{25,1},{2,10},{10... | collective-permute-start | bytes 36872 | tf_op jit(solution)/shard_map/ppermute | solution.py:16
  27.3 3.1 %collective-permute-start.4 = (f32[3,1,8,128]{3,2,1,0:T(8,128)S(1)}, f32[3,1,8,128]{3,2,1,0:T(8,128)S(1)}, u32[]{:S(2)}, u32[]{:S(2)}) collective-permute-start(f32[3,1,8,128]{3,2,1,0:T(8,128)S(1)} %get-tuple-element.46), channel_id=1, source_target_pairs={{8,0},{16,8},{24,16},{0,24},{9,1},{17,9},{25,17},{1,25},{10,2},{18... | collective-permute-start | bytes 36872 | tf_op jit(solution)/shard_map/ppermute | solution.py:19
  30.4 3.8 %collective-permute-start.6 = (f32[3,10,1,128]{3,2,1,0:T(1,128)S(1)}, f32[3,10,1,128]{3,2,1,0:T(1,128)S(1)}, u32[]{:S(2)}, u32[]{:S(2)}) collective-permute-start(f32[3,10,1,128]{3,2,1,0:T(1,128)S(1)} %get-tuple-element.29), channel_id=1, source_target_pairs={{1,0},{2,1},{3,2},{4,3},{5,4},{6,5},{7,6},{0,7},{9,8},{10,9},{11,1... | collective-permute-start | bytes 46088 | tf_op jit(solution)/shard_map/ppermute | solution.py:19
  30.5 6.5 %collective-permute-start.7 = (f32[3,10,1,128]{3,2,1,0:T(1,128)S(1)}, f32[3,10,1,128]{3,2,1,0:T(1,128)S(1)}, u32[]{:S(2)}, u32[]{:S(2)}) collective-permute-start(f32[3,10,1,128]{3,2,1,0:T(1,128)S(1)} %get-tuple-element.30), channel_id=1, source_target_pairs={{0,1},{1,2},{2,3},{3,4},{4,5},{5,6},{6,7},{7,0},{8,9},{9,10},{10,1... | collective-permute-start | bytes 46088 | tf_op jit(solution)/shard_map/ppermute | solution.py:16
  116.6 3.2 %collective-permute-start.9 = (f32[3,1,8,128]{3,2,1,0:T(8,128)S(1)}, f32[3,1,8,128]{3,2,1,0:T(8,128)S(1)}, u32[]{:S(2)}, u32[]{:S(2)}) collective-permute-start(f32[3,1,8,128]{3,2,1,0:T(8,128)S(1)} %get-tuple-element.39), channel_id=1, source_target_pairs={{0,8},{8,16},{16,24},{24,0},{1,9},{9,17},{17,25},{25,1},{2,10},{10... | collective-permute-start | bytes 36872 | tf_op jit(solution)/shard_map/ppermute | solution.py:16
  116.7 3.1 %collective-permute-start.8 = (f32[3,1,8,128]{3,2,1,0:T(8,128)S(1)}, f32[3,1,8,128]{3,2,1,0:T(8,128)S(1)}, u32[]{:S(2)}, u32[]{:S(2)}) collective-permute-start(f32[3,1,8,128]{3,2,1,0:T(8,128)S(1)} %get-tuple-element.40), channel_id=1, source_target_pairs={{8,0},{16,8},{24,16},{0,24},{9,1},{17,9},{25,17},{1,25},{10,2},{18... | collective-permute-start | bytes 36872 | tf_op jit(solution)/shard_map/ppermute | solution.py:19
  119.9 4.7 %collective-permute-start.10 = (f32[3,10,1,128]{3,2,1,0:T(1,128)S(1)}, f32[3,10,1,128]{3,2,1,0:T(1,128)S(1)}, u32[]{:S(2)}, u32[]{:S(2)}) collective-permute-start(f32[3,10,1,128]{3,2,1,0:T(1,128)S(1)} %get-tuple-element.27), channel_id=1, source_target_pairs={{1,0},{2,1},{3,2},{4,3},{5,4},{6,5},{7,6},{0,7},{9,8},{10,9},{11,1... | collective-permute-start | bytes 46088 | tf_op jit(solution)/shard_map/ppermute | solution.py:19
  123.2 6.4 %collective-permute-start.11 = (f32[3,10,1,128]{3,2,1,0:T(1,128)S(1)}, f32[3,10,1,128]{3,2,1,0:T(1,128)S(1)}, u32[]{:S(2)}, u32[]{:S(2)}) collective-permute-start(f32[3,10,1,128]{3,2,1,0:T(1,128)S(1)} %get-tuple-element.28), channel_id=1, source_target_pairs={{0,1},{1,2},{2,3},{3,4},{4,5},{5,6},{6,7},{7,0},{8,9},{9,10},{10,1... | collective-permute-start | bytes 46088 | tf_op jit(solution)/shard_map/ppermute | solution.py:16
  208.4 3.2 %collective-permute-start.13 = (f32[3,1,8,128]{3,2,1,0:T(8,128)S(1)}, f32[3,1,8,128]{3,2,1,0:T(8,128)S(1)}, u32[]{:S(2)}, u32[]{:S(2)}) collective-permute-start(f32[3,1,8,128]{3,2,1,0:T(8,128)S(1)} %get-tuple-element.37), channel_id=1, source_target_pairs={{0,8},{8,16},{16,24},{24,0},{1,9},{9,17},{17,25},{25,1},{2,10},{10... | collective-permute-start | bytes 36872 | tf_op jit(solution)/shard_map/ppermute | solution.py:16
  208.5 3.1 %collective-permute-start.12 = (f32[3,1,8,128]{3,2,1,0:T(8,128)S(1)}, f32[3,1,8,128]{3,2,1,0:T(8,128)S(1)}, u32[]{:S(2)}, u32[]{:S(2)}) collective-permute-start(f32[3,1,8,128]{3,2,1,0:T(8,128)S(1)} %get-tuple-element.38), channel_id=1, source_target_pairs={{8,0},{16,8},{24,16},{0,24},{9,1},{17,9},{25,17},{1,25},{10,2},{18... | collective-permute-start | bytes 36872 | tf_op jit(solution)/shard_map/ppermute | solution.py:19
  211.7 4.7 %collective-permute-start.14 = (f32[3,10,1,128]{3,2,1,0:T(1,128)S(1)}, f32[3,10,1,128]{3,2,1,0:T(1,128)S(1)}, u32[]{:S(2)}, u32[]{:S(2)}) collective-permute-start(f32[3,10,1,128]{3,2,1,0:T(1,128)S(1)} %get-tuple-element.25), channel_id=1, source_target_pairs={{1,0},{2,1},{3,2},{4,3},{5,4},{6,5},{7,6},{0,7},{9,8},{10,9},{11,1... | collective-permute-start | bytes 46088 | tf_op jit(solution)/shard_map/ppermute | solution.py:19
  215.0 6.4 %collective-permute-start.15 = (f32[3,10,1,128]{3,2,1,0:T(1,128)S(1)}, f32[3,10,1,128]{3,2,1,0:T(1,128)S(1)}, u32[]{:S(2)}, u32[]{:S(2)}) collective-permute-start(f32[3,10,1,128]{3,2,1,0:T(1,128)S(1)} %get-tuple-element.26), channel_id=1, source_target_pairs={{0,1},{1,2},{2,3},{3,4},{4,5},{5,6},{6,7},{7,0},{8,9},{9,10},{10,1... | collective-permute-start | bytes 46088 | tf_op jit(solution)/shard_map/ppermute | solution.py:16
  258.6 18.3 %copy-start.1 = (f32[3,8,8,128]{3,2,1,0:T(8,128)}, f32[3,8,8,128]{3,2,1,0:T(8,128)S(1)}, u32[]{:S(2)}) copy-start(f32[3,8,8,128]{3,2,1,0:T(8,128)S(1)} %multiply_add_fusion) | copy-start | bytes 294916
  258.7 7.7 %collective-permute-start.17 = (f32[3,1,8,128]{3,2,1,0:T(8,128)S(1)}, f32[3,1,8,128]{3,2,1,0:T(8,128)S(1)}, u32[]{:S(2)}, u32[]{:S(2)}) collective-permute-start(f32[3,1,8,128]{3,2,1,0:T(8,128)S(1)} %get-tuple-element.31), channel_id=1, source_target_pairs={{0,8},{8,16},{16,24},{24,0},{1,9},{9,17},{17,25},{25,1},{2,10},{10... | collective-permute-start | bytes 36872 | tf_op jit(solution)/shard_map/ppermute | solution.py:16
  258.8 7.6 %collective-permute-start.16 = (f32[3,1,8,128]{3,2,1,0:T(8,128)S(1)}, f32[3,1,8,128]{3,2,1,0:T(8,128)S(1)}, u32[]{:S(2)}, u32[]{:S(2)}) collective-permute-start(f32[3,1,8,128]{3,2,1,0:T(8,128)S(1)} %get-tuple-element.32), channel_id=1, source_target_pairs={{8,0},{16,8},{24,16},{0,24},{9,1},{17,9},{25,17},{1,25},{10,2},{18... | collective-permute-start | bytes 36872 | tf_op jit(solution)/shard_map/ppermute | solution.py:19
  266.4 9.7 %collective-permute-start.18 = (f32[3,10,1,128]{3,2,1,0:T(1,128)S(1)}, f32[3,10,1,128]{3,2,1,0:T(1,128)S(1)}, u32[]{:S(2)}, u32[]{:S(2)}) collective-permute-start(f32[3,10,1,128]{3,2,1,0:T(1,128)S(1)} %get-tuple-element.23), channel_id=1, source_target_pairs={{1,0},{2,1},{3,2},{4,3},{5,4},{6,5},{7,6},{0,7},{9,8},{10,9},{11,1... | collective-permute-start | bytes 46088 | tf_op jit(solution)/shard_map/ppermute | solution.py:19
  270.5 6.4 %collective-permute-start.19 = (f32[3,10,1,128]{3,2,1,0:T(1,128)S(1)}, f32[3,10,1,128]{3,2,1,0:T(1,128)S(1)}, u32[]{:S(2)}, u32[]{:S(2)}) collective-permute-start(f32[3,10,1,128]{3,2,1,0:T(1,128)S(1)} %get-tuple-element.24), channel_id=1, source_target_pairs={{0,1},{1,2},{2,3},{3,4},{4,5},{5,6},{6,7},{7,0},{8,9},{9,10},{10,1... | collective-permute-start | bytes 46088 | tf_op jit(solution)/shard_map/ppermute | solution.py:16
where the time goes:
time: 285 us; the launch traced here: 283 us
  blocking collectives  194 us (68%)
  other arithmetic  28.3 us (10%)
  waiting for transfers between devices  28.3 us (10%)
  starting transfers between devices  27.8 us (10%)
  local copies, waits for them, and re-layouts  3.7 us (1%)
    psum x3, blocking collectives, squares(): lax.psum(jnp.sum(residual * residual, axis=(1, 2, 3)), ('col', 'slab'))  121 us
    psum x2, blocking collectives, shards(): lax.psum(jnp.sum(direction * image, axis=(1, 2, 3)), ('col', 'slab'))  73.7 us
    ppermute x10, starting transfers between devices, extended(): lax.ppermute(lax.slice_in_dim(block, 0, width, axis=dim), axis, backward)  25 us
    ppermute x10, waiting for transfers between devices, extended(): lax.ppermute(lax.slice_in_dim(block, block.shape[dim] - width, None, axis...  22.4 us
    sub x2, other arithmetic, shards(): energy - (lam_diff[0] * local[0] + lam_diff[1] * local[1] + lam_diff[2] *...  11.4 us
    ppermute x10, waiting for transfers between devices, extended(): lax.ppermute(lax.slice_in_dim(block, 0, width, axis=dim), axis, backward)  5.95 us
    mul x1, other arithmetic, shards(): unused_now, term_prev = split_faces(h_term * part_after, d)  5.72 us
  transfers between devices with their start and end apart: 20, of which 12 were waited for; matrix products, arithmetic and copies ran while one was open for 5% of the time, Pallas kernels for 0%

commit v1 on v0

--- a/solution.py
+++ b/solution.py
@@ -94,7 +94,7 @@
     for step in range(ITERS):
         dir_pad = extended(direction, (("col", 1), ("slab", 2)), 1)
         image = apply_operator(dir_pad, direction, cond_full)
-        curve = lax.psum(jnp.sum(direction * image, axis=(1, 2, 3)), ("col", "slab"))
+        curve = lax.psum(lax.psum(jnp.sum(direction * image, axis=(1, 2, 3)), "slab"), "col")
         alpha = norm_now / curve
         adjoint = adjoint + widen(alpha) * direction
         residual = residual - widen(alpha) * image

time: 285 us -> 276 us (0.968)
  blocking collectives: 194 us -> 187 us
    psum x2 -> x6, blocking collectives: 73.7 us -> 68.4 us  [the longest x3 51.3 us: shards(): lax.psum(jnp.sum(direction * image, axis=(1, 2, 3)), 'slab')]
where the time goes in v1:
time: 276 us; the launch traced here: 275 us
  blocking collectives  187 us (68%)
  waiting for transfers between devices  28.3 us (10%)
  other arithmetic  28.1 us (10%)
  starting transfers between devices  26.6 us (10%)
  local copies, waits for them, and re-layouts  3.69 us (1%)
    psum x3, blocking collectives, squares(): lax.psum(jnp.sum(residual * residual, axis=(1, 2, 3)), ('col', 'slab'))  118 us
    psum x3, blocking collectives, shards(): lax.psum(jnp.sum(direction * image, axis=(1, 2, 3)), 'slab')  51.3 us
    ppermute x10, starting transfers between devices, extended(): lax.ppermute(lax.slice_in_dim(block, 0, width, axis=dim), axis, backward)  23.8 us
    ppermute x10, waiting for transfers between devices, extended(): lax.ppermute(lax.slice_in_dim(block, block.shape[dim] - width, None, axis...  22.4 us
    psum x3, blocking collectives, shards(): lax.psum(lax.psum(jnp.sum(direction * image, axis=(1, 2, 3)), 'slab'), 'c...  17 us
    sub x2, other arithmetic, shards(): energy - (lam_diff[0] * local[0] + lam_diff[1] * local[1] + lam_diff[2] *...  11.3 us
    ppermute x10, waiting for transfers between devices, extended(): lax.ppermute(lax.slice_in_dim(block, 0, width, axis=dim), axis, backward)  5.95 us
    mul x1, other arithmetic, shards(): unused_now, term_prev = split_faces(h_term * part_after, d)  5.67 us
  transfers between devices with their start and end apart: 20, of which 12 were waited for; matrix products, arithmetic and copies ran while one was open for 5% of the time, Pallas kernels for 0%

profile of v1, /device:TPU:0, one launch (start us, length us, event | category | flops | bytes accessed | tf_op | source)
XLA Modules:
  0.0 274.5 jit_solution(13815061697196058793)
XLA Ops:
  0.6 1.3 fusion.147
  2.0 2.6 select_multiply_fusion
  5.1 2.0 collective-permute-start.1
  9.1 5.4 %collective-permute-start.3 = (f32[4,10,1,128]{3,2,1,0:T(1,128)S(1)}, f32[4,10,1,128]{3,2,1,0:T(1,128)S(1)}, u32[]{:S(2)}, u32[]{:S(2)}) collective-permute-start(f32[4,10,1,128]{3,2,1,0:T(1,128)S(1)} %get-tuple-element.17), channel_id=1, source_target_pairs={{1,0},{2,1},{3,2},{4,3},{5,4},{6,5},{7,6},{0,7},{9,8},{10,9},{11,1... | collective-permute-start | bytes 61448 | tf_op jit(solution)/shard_map/ppermute | solution.py:19
  14.5 1.5 collective-permute-done.3
  15.9 5.1 %collective-permute-done.2 = f32[4,10,1,128]{3,2,1,0:T(1,128)S(1)} collective-permute-done((f32[4,10,1,128]{3,2,1,0:T(1,128)S(1)}, f32[4,10,1,128]{3,2,1,0:T(1,128)S(1)}, u32[]{:S(2)}, u32[]{:S(2)}) %collective-permute-start.2) | collective-permute-done | bytes 20512 | tf_op jit(solution)/shard_map/ppermute | solution.py:16
  21.3 5.6 %multiply_add_fusion.5 = (f32[1,8,8,128]{3,2,1,0:T(8,128)S(1)}, f32[1,8,8,128]{3,2,1,0:T(8,128)S(1)}, f32[1,8,8,128]{3,2,1,0:T(8,128)S(1)}) fusion(f32[3,8,8,128]{3,2,1,0:T(8,128)S(1)} %fusion.46, f32[]{:T(128)} %bitcast.7, f32[]{:T(128)} %bitcast.6, f32[]{:T(128)} %bitcast, f32[]{:T(128)} %bitcast.10, f32[]{:T(128)} %bitcast.9, f32[]{:T(128)} %bitcast.8, ...), kind=kLoop, calls=%fused_computation.280 | loop fusion | flops 122880 | bytes 196644 | tf_op jit(solution)/shard_map/add | solution.py:86
  27.2 1.7 collective-permute-start.4
  30.4 2.0 collective-permute-start.7
  32.5 1.7 collective-permute-done.6
  34.2 2.8 %collective-permute-done.7 = f32[3,10,1,128]{3,2,1,0:T(1,128)S(1)} collective-permute-done((f32[3,10,1,128]{3,2,1,0:T(1,128)S(1)}, f32[3,10,1,128]{3,2,1,0:T(1,128)S(1)}, u32[]{:S(2)}, u32[]{:S(2)}) %collective-permute-start.7) | collective-permute-done | bytes 15392 | tf_op jit(solution)/shard_map/ppermute | solution.py:16
  37.2 17.1 %psum.64 = f32[3]{0:T(128)S(1)} all-reduce(f32[3]{0:T(128)S(1)} %get-tuple-element.2), channel_id=1, replica_groups=mesh['col'=4,'slab'=8] {'slab'}, use_global_device_ids=true, to_apply=%region_3.4 | all-reduce | flops 3 | bytes 24 | tf_op jit(solution)/shard_map/psum | solution.py:97
  54.3 5.6 %psum.65 = f32[3]{0:T(128)S(1)} all-reduce(f32[3]{0:T(128)S(1)} %psum.64), channel_id=1, replica_groups=mesh['col'=4,'slab'=8] {'col'}, use_global_device_ids=true, to_apply=%region_4.5 | all-reduce | flops 3 | bytes 24 | tf_op jit(solution)/shard_map/psum | solution.py:97
  59.9 38.6 %psum.63 = f32[3]{0:T(128)S(1)} all-reduce(f32[3]{0:T(128)S(1)} %get-tuple-element.3), channel_id=1, replica_groups=mesh['col'=4,'slab'=8] {'col','slab'}, use_global_device_ids=true, to_apply=%region_1.2 | all-reduce | flops 3 | bytes 24 | tf_op jit(solution)/shard_map/psum | solution.py:62
  98.8 41.1 %psum.66 = f32[3]{0:T(128)S(1)} all-reduce(f32[3]{0:T(128)S(1)} %get-tuple-element.8), channel_id=1, replica_groups=mesh['col'=4,'slab'=8] {'col','slab'}, use_global_device_ids=true, to_apply=%region_6.7 | all-reduce | flops 3 | bytes 24 | tf_op jit(solution)/shard_map/psum | solution.py:62
  140.0 1.7 collective-permute-start.8
  143.2 3.3 %collective-permute-start.10 = (f32[3,10,1,128]{3,2,1,0:T(1,128)S(1)}, f32[3,10,1,128]{3,2,1,0:T(1,128)S(1)}, u32[]{:S(2)}, u32[]{:S(2)}) collective-permute-start(f32[3,10,1,128]{3,2,1,0:T(1,128)S(1)} %get-tuple-element.25), channel_id=1, source_target_pairs={{1,0},{2,1},{3,2},{4,3},{5,4},{6,5},{7,6},{0,7},{9,8},{10,9},{11,1... | collective-permute-start | bytes 46088 | tf_op jit(solution)/shard_map/ppermute | solution.py:19
  146.6 1.3 collective-permute-done.10
  147.9 5.0 %collective-permute-done.11 = f32[3,10,1,128]{3,2,1,0:T(1,128)S(1)} collective-permute-done((f32[3,10,1,128]{3,2,1,0:T(1,128)S(1)}, f32[3,10,1,128]{3,2,1,0:T(1,128)S(1)}, u32[]{:S(2)}, u32[]{:S(2)}) %collective-permute-start.11) | collective-permute-done | bytes 15392 | tf_op jit(solution)/shard_map/ppermute | solution.py:16
  153.1 17.1 %psum.67 = f32[3]{0:T(128)S(1)} all-reduce(f32[3]{0:T(128)S(1)} %get-tuple-element.6), channel_id=1, replica_groups=mesh['col'=4,'slab'=8] {'slab'}, use_global_device_ids=true, to_apply=%region_8.9 | all-reduce | flops 3 | bytes 24 | tf_op jit(solution)/shard_map/psum | solution.py:97
  170.3 5.6 %psum.68 = f32[3]{0:T(128)S(1)} all-reduce(f32[3]{0:T(128)S(1)} %psum.67), channel_id=1, replica_groups=mesh['col'=4,'slab'=8] {'col'}, use_global_device_ids=true, to_apply=%region_9.10 | all-reduce | flops 3 | bytes 24 | tf_op jit(solution)/shard_map/psum | solution.py:97
  176.1 38.7 %psum.69 = f32[3]{0:T(128)S(1)} all-reduce(f32[3]{0:T(128)S(1)} %multiply_reduce_fusion), channel_id=1, replica_groups=mesh['col'=4,'slab'=8] {'col','slab'}, use_global_device_ids=true, to_apply=%region_11.12 | all-reduce | flops 3 | bytes 24 | tf_op jit(solution)/shard_map/psum | solution.py:62
  215.0 1.7 collective-permute-start.12
  218.2 4.0 %collective-permute-start.14 = (f32[3,10,1,128]{3,2,1,0:T(1,128)S(1)}, f32[3,10,1,128]{3,2,1,0:T(1,128)S(1)}, u32[]{:S(2)}, u32[]{:S(2)}) collective-permute-start(f32[3,10,1,128]{3,2,1,0:T(1,128)S(1)} %get-tuple-element.23), channel_id=1, source_target_pairs={{1,0},{2,1},{3,2},{4,3},{5,4},{6,5},{7,6},{0,7},{9,8},{10,9},{11,1... | collective-permute-start | bytes 46088 | tf_op jit(solution)/shard_map/ppermute | solution.py:19
  223.6 5.0 %collective-permute-done.15 = f32[3,10,1,128]{3,2,1,0:T(1,128)S(1)} collective-permute-done((f32[3,10,1,128]{3,2,1,0:T(1,128)S(1)}, f32[3,10,1,128]{3,2,1,0:T(1,128)S(1)}, u32[]{:S(2)}, u32[]{:S(2)}) %collective-permute-start.15) | collective-permute-done | bytes 15392 | tf_op jit(solution)/shard_map/ppermute | solution.py:16
  228.9 17.1 %psum.70 = f32[3]{0:T(128)S(1)} all-reduce(f32[3]{0:T(128)S(1)} %fusion.7), channel_id=1, replica_groups=mesh['col'=4,'slab'=8] {'slab'}, use_global_device_ids=true, to_apply=%region_13.14 | all-reduce | flops 3 | bytes 24 | tf_op jit(solution)/shard_map/psum | solution.py:97
  246.0 5.7 %psum.71 = f32[3]{0:T(128)S(1)} all-reduce(f32[3]{0:T(128)S(1)} %psum.70), channel_id=1, replica_groups=mesh['col'=4,'slab'=8] {'col'}, use_global_device_ids=true, to_apply=%region_14.15 | all-reduce | flops 3 | bytes 24 | tf_op jit(solution)/shard_map/psum | solution.py:97
  252.0 1.7 collective-permute-start.16
  253.8 5.7 %fusion.94 = (f32[8,8,128]{2,1,0:T(8,128)S(1)}, f32[8,8,128]{2,1,0:T(8,128)S(1)}) fusion(f32[8,8,128]{2,1,0:T(8,128)S(1)} %select_multiply_fusion, f32[8,8,1]{2,1,0:T(8,128)S(1)} %bitcast.219, f32[8,8,127]{2,1,0:T(8,128)S(1)} %slice.582, f32[3,8,8,128]{3,2,1,0:T(8,128)S(1)} %maximum_subtract_fusion.8, f32[]{:T(128)} %bitcast.13, f32[]{:T(128)} %bitcast.12, ...), kind=kLoop, calls=%fused_computation.222 | loop fusion | flops 319488 | bytes 327716 | tf_op jit(solution)/shard_map/mul | solution.py:120
  259.6 2.1 collective-permute-start.18
  261.8 5.6 %fusion.81 = f32[9,8,128]{2,1,0:T(8,128)S(1)} fusion(f32[3,9,8,128]{3,2,1,0:T(8,128)S(1)} %maximum_subtract_fusion, f32[1,9,8,128]{3,2,1,0:T(8,128)S(1)} %get-tuple-element.16, f32[1,9,8,128]{3,2,1,0:T(8,128)S(1)} %get-tuple-element.15, f32[1,9,8,128]{3,2,1,0:T(8,128)S(1)} %get-tuple-element.14, f32[]{:T(128)} %bitcast.13, f32[]{:T(128)} %bitcast.12, ...), kind=kLoop, calls=%fused_computation.190 | loop fusion | flops 294912 | bytes 258084 | tf_op jit(solution)/shard_map/sub | solution.py:114
  268.2 5.7 %fusion.62 = f32[8,9,128]{2,1,0:T(8,128)S(1)} fusion(f32[3,8,9,128]{3,2,1,0:T(8,128)S(1)} %fusion, f32[1,8,9,128]{3,2,1,0:T(8,128)S(1)} %fusion.68, f32[1,8,9,128]{3,2,1,0:T(8,128)S(1)} %fusion.69, f32[1,8,9,128]{3,2,1,0:T(8,128)S(1)} %maximum_subtract_fusion.10, f32[]{:T(128)} %bitcast.13, f32[]{:T(128)} %bitcast.12, f32[]{:T(128)} %bitcast.11, ...), kind=kLoop, calls=%fused_computation.137 | loop fusion | flops 294912 | bytes 258084 | tf_op jit(solution)/shard_map/sub | solution.py:114
  (85 shorter events, 12.1 us)
Async XLA Ops:
  0.6 4.0 %copy-start = (f32[3,8,8,128]{3,2,1,0:T(8,128)S(1)}, f32[3,8,8,128]{3,2,1,0:T(8,128)}, u32[]{:S(2)}) copy-start(f32[3,8,8,128]{3,2,1,0:T(8,128)} %param.8) | copy-start | bytes 294916
  4.6 4.4 %collective-permute-start = (f32[4,1,8,128]{3,2,1,0:T(8,128)S(1)}, f32[4,1,8,128]{3,2,1,0:T(8,128)S(1)}, u32[]{:S(2)}, u32[]{:S(2)}) collective-permute-start(f32[4,1,8,128]{3,2,1,0:T(8,128)S(1)} %get-tuple-element.19), channel_id=1, source_target_pairs={{0,8},{8,16},{16,24},{24,0},{1,9},{9,17},{17,25},{25,1},{2,10},{10... | collective-permute-start | bytes 49160 | tf_op jit(solution)/shard_map/ppermute | solution.py:16
  5.1 3.9 %collective-permute-start.1 = (f32[4,1,8,128]{3,2,1,0:T(8,128)S(1)}, f32[4,1,8,128]{3,2,1,0:T(8,128)S(1)}, u32[]{:S(2)}, u32[]{:S(2)}) collective-permute-start(f32[4,1,8,128]{3,2,1,0:T(8,128)S(1)} %get-tuple-element.20), channel_id=1, source_target_pairs={{8,0},{16,8},{24,16},{0,24},{9,1},{17,9},{25,17},{1,25},{10,2},{18... | collective-permute-start | bytes 49160 | tf_op jit(solution)/shard_map/ppermute | solution.py:19
  7.5 0.7 copy-start.2
  9.1 6.8 %collective-permute-start.3 = (f32[4,10,1,128]{3,2,1,0:T(1,128)S(1)}, f32[4,10,1,128]{3,2,1,0:T(1,128)S(1)}, u32[]{:S(2)}, u32[]{:S(2)}) collective-permute-start(f32[4,10,1,128]{3,2,1,0:T(1,128)S(1)} %get-tuple-element.17), channel_id=1, source_target_pairs={{1,0},{2,1},{3,2},{4,3},{5,4},{6,5},{7,6},{0,7},{9,8},{10,9},{11,1... | collective-permute-start | bytes 61448 | tf_op jit(solution)/shard_map/ppermute | solution.py:19
  14.4 6.6 %collective-permute-start.2 = (f32[4,10,1,128]{3,2,1,0:T(1,128)S(1)}, f32[4,10,1,128]{3,2,1,0:T(1,128)S(1)}, u32[]{:S(2)}, u32[]{:S(2)}) collective-permute-start(f32[4,10,1,128]{3,2,1,0:T(1,128)S(1)} %get-tuple-element.18), channel_id=1, source_target_pairs={{0,1},{1,2},{2,3},{3,4},{4,5},{5,6},{6,7},{7,0},{8,9},{9,10},{10,1... | collective-permute-start | bytes 61448 | tf_op jit(solution)/shard_map/ppermute | solution.py:16
  27.1 3.2 %collective-permute-start.5 = (f32[3,1,8,128]{3,2,1,0:T(8,128)S(1)}, f32[3,1,8,128]{3,2,1,0:T(8,128)S(1)}, u32[]{:S(2)}, u32[]{:S(2)}) collective-permute-start(f32[3,1,8,128]{3,2,1,0:T(8,128)S(1)} %get-tuple-element.43), channel_id=1, source_target_pairs={{0,8},{8,16},{16,24},{24,0},{1,9},{9,17},{17,25},{25,1},{2,10},{10... | collective-permute-start | bytes 36872 | tf_op jit(solution)/shard_map/ppermute | solution.py:16
  27.2 3.1 %collective-permute-start.4 = (f32[3,1,8,128]{3,2,1,0:T(8,128)S(1)}, f32[3,1,8,128]{3,2,1,0:T(8,128)S(1)}, u32[]{:S(2)}, u32[]{:S(2)}) collective-permute-start(f32[3,1,8,128]{3,2,1,0:T(8,128)S(1)} %get-tuple-element.44), channel_id=1, source_target_pairs={{8,0},{16,8},{24,16},{0,24},{9,1},{17,9},{25,17},{1,25},{10,2},{18... | collective-permute-start | bytes 36872 | tf_op jit(solution)/shard_map/ppermute | solution.py:19
  30.4 3.8 %collective-permute-start.6 = (f32[3,10,1,128]{3,2,1,0:T(1,128)S(1)}, f32[3,10,1,128]{3,2,1,0:T(1,128)S(1)}, u32[]{:S(2)}, u32[]{:S(2)}) collective-permute-start(f32[3,10,1,128]{3,2,1,0:T(1,128)S(1)} %get-tuple-element.27), channel_id=1, source_target_pairs={{1,0},{2,1},{3,2},{4,3},{5,4},{6,5},{7,6},{0,7},{9,8},{10,9},{11,1... | collective-permute-start | bytes 46088 | tf_op jit(solution)/shard_map/ppermute | solution.py:19
  30.4 6.5 %collective-permute-start.7 = (f32[3,10,1,128]{3,2,1,0:T(1,128)S(1)}, f32[3,10,1,128]{3,2,1,0:T(1,128)S(1)}, u32[]{:S(2)}, u32[]{:S(2)}) collective-permute-start(f32[3,10,1,128]{3,2,1,0:T(1,128)S(1)} %get-tuple-element.28), channel_id=1, source_target_pairs={{0,1},{1,2},{2,3},{3,4},{4,5},{5,6},{6,7},{7,0},{8,9},{9,10},{10,1... | collective-permute-start | bytes 46088 | tf_op jit(solution)/shard_map/ppermute | solution.py:16
  139.9 3.2 %collective-permute-start.9 = (f32[3,1,8,128]{3,2,1,0:T(8,128)S(1)}, f32[3,1,8,128]{3,2,1,0:T(8,128)S(1)}, u32[]{:S(2)}, u32[]{:S(2)}) collective-permute-start(f32[3,1,8,128]{3,2,1,0:T(8,128)S(1)} %get-tuple-element.37), channel_id=1, source_target_pairs={{0,8},{8,16},{16,24},{24,0},{1,9},{9,17},{17,25},{25,1},{2,10},{10... | collective-permute-start | bytes 36872 | tf_op jit(solution)/shard_map/ppermute | solution.py:16
  140.0 3.1 %collective-permute-start.8 = (f32[3,1,8,128]{3,2,1,0:T(8,128)S(1)}, f32[3,1,8,128]{3,2,1,0:T(8,128)S(1)}, u32[]{:S(2)}, u32[]{:S(2)}) collective-permute-start(f32[3,1,8,128]{3,2,1,0:T(8,128)S(1)} %get-tuple-element.38), channel_id=1, source_target_pairs={{8,0},{16,8},{24,16},{0,24},{9,1},{17,9},{25,17},{1,25},{10,2},{18... | collective-permute-start | bytes 36872 | tf_op jit(solution)/shard_map/ppermute | solution.py:19
  143.2 4.8 %collective-permute-start.10 = (f32[3,10,1,128]{3,2,1,0:T(1,128)S(1)}, f32[3,10,1,128]{3,2,1,0:T(1,128)S(1)}, u32[]{:S(2)}, u32[]{:S(2)}) collective-permute-start(f32[3,10,1,128]{3,2,1,0:T(1,128)S(1)} %get-tuple-element.25), channel_id=1, source_target_pairs={{1,0},{2,1},{3,2},{4,3},{5,4},{6,5},{7,6},{0,7},{9,8},{10,9},{11,1... | collective-permute-start | bytes 46088 | tf_op jit(solution)/shard_map/ppermute | solution.py:19
  146.5 6.4 %collective-permute-start.11 = (f32[3,10,1,128]{3,2,1,0:T(1,128)S(1)}, f32[3,10,1,128]{3,2,1,0:T(1,128)S(1)}, u32[]{:S(2)}, u32[]{:S(2)}) collective-permute-start(f32[3,10,1,128]{3,2,1,0:T(1,128)S(1)} %get-tuple-element.26), channel_id=1, source_target_pairs={{0,1},{1,2},{2,3},{3,4},{4,5},{5,6},{6,7},{7,0},{8,9},{9,10},{10,1... | collective-permute-start | bytes 46088 | tf_op jit(solution)/shard_map/ppermute | solution.py:16
  214.9 3.2 %collective-permute-start.13 = (f32[3,1,8,128]{3,2,1,0:T(8,128)S(1)}, f32[3,1,8,128]{3,2,1,0:T(8,128)S(1)}, u32[]{:S(2)}, u32[]{:S(2)}) collective-permute-start(f32[3,1,8,128]{3,2,1,0:T(8,128)S(1)} %get-tuple-element.35), channel_id=1, source_target_pairs={{0,8},{8,16},{16,24},{24,0},{1,9},{9,17},{17,25},{25,1},{2,10},{10... | collective-permute-start | bytes 36872 | tf_op jit(solution)/shard_map/ppermute | solution.py:16
  215.0 3.1 %collective-permute-start.12 = (f32[3,1,8,128]{3,2,1,0:T(8,128)S(1)}, f32[3,1,8,128]{3,2,1,0:T(8,128)S(1)}, u32[]{:S(2)}, u32[]{:S(2)}) collective-permute-start(f32[3,1,8,128]{3,2,1,0:T(8,128)S(1)} %get-tuple-element.36), channel_id=1, source_target_pairs={{8,0},{16,8},{24,16},{0,24},{9,1},{17,9},{25,17},{1,25},{10,2},{18... | collective-permute-start | bytes 36872 | tf_op jit(solution)/shard_map/ppermute | solution.py:19
  218.2 5.5 %collective-permute-start.14 = (f32[3,10,1,128]{3,2,1,0:T(1,128)S(1)}, f32[3,10,1,128]{3,2,1,0:T(1,128)S(1)}, u32[]{:S(2)}, u32[]{:S(2)}) collective-permute-start(f32[3,10,1,128]{3,2,1,0:T(1,128)S(1)} %get-tuple-element.23), channel_id=1, source_target_pairs={{1,0},{2,1},{3,2},{4,3},{5,4},{6,5},{7,6},{0,7},{9,8},{10,9},{11,1... | collective-permute-start | bytes 46088 | tf_op jit(solution)/shard_map/ppermute | solution.py:19
  222.2 6.4 %collective-permute-start.15 = (f32[3,10,1,128]{3,2,1,0:T(1,128)S(1)}, f32[3,10,1,128]{3,2,1,0:T(1,128)S(1)}, u32[]{:S(2)}, u32[]{:S(2)}) collective-permute-start(f32[3,10,1,128]{3,2,1,0:T(1,128)S(1)} %get-tuple-element.24), channel_id=1, source_target_pairs={{0,1},{1,2},{2,3},{3,4},{4,5},{5,6},{6,7},{7,0},{8,9},{9,10},{10,1... | collective-permute-start | bytes 46088 | tf_op jit(solution)/shard_map/ppermute | solution.py:16
  251.8 16.3 %copy-start.1 = (f32[3,8,8,128]{3,2,1,0:T(8,128)}, f32[3,8,8,128]{3,2,1,0:T(8,128)S(1)}, u32[]{:S(2)}) copy-start(f32[3,8,8,128]{3,2,1,0:T(8,128)S(1)} %multiply_add_fusion) | copy-start | bytes 294916
  251.9 7.7 %collective-permute-start.17 = (f32[3,1,8,128]{3,2,1,0:T(8,128)S(1)}, f32[3,1,8,128]{3,2,1,0:T(8,128)S(1)}, u32[]{:S(2)}, u32[]{:S(2)}) collective-permute-start(f32[3,1,8,128]{3,2,1,0:T(8,128)S(1)} %get-tuple-element.29), channel_id=1, source_target_pairs={{0,8},{8,16},{16,24},{24,0},{1,9},{9,17},{17,25},{25,1},{2,10},{10... | collective-permute-start | bytes 36872 | tf_op jit(solution)/shard_map/ppermute | solution.py:16
  252.0 7.6 %collective-permute-start.16 = (f32[3,1,8,128]{3,2,1,0:T(8,128)S(1)}, f32[3,1,8,128]{3,2,1,0:T(8,128)S(1)}, u32[]{:S(2)}, u32[]{:S(2)}) collective-permute-start(f32[3,1,8,128]{3,2,1,0:T(8,128)S(1)} %get-tuple-element.30), channel_id=1, source_target_pairs={{8,0},{16,8},{24,16},{0,24},{9,1},{17,9},{25,17},{1,25},{10,2},{18... | collective-permute-start | bytes 36872 | tf_op jit(solution)/shard_map/ppermute | solution.py:19
  259.6 7.8 %collective-permute-start.18 = (f32[3,10,1,128]{3,2,1,0:T(1,128)S(1)}, f32[3,10,1,128]{3,2,1,0:T(1,128)S(1)}, u32[]{:S(2)}, u32[]{:S(2)}) collective-permute-start(f32[3,10,1,128]{3,2,1,0:T(1,128)S(1)} %get-tuple-element.21), channel_id=1, source_target_pairs={{1,0},{2,1},{3,2},{4,3},{5,4},{6,5},{7,6},{0,7},{9,8},{10,9},{11,1... | collective-permute-start | bytes 46088 | tf_op jit(solution)/shard_map/ppermute | solution.py:19
  261.7 6.4 %collective-permute-start.19 = (f32[3,10,1,128]{3,2,1,0:T(1,128)S(1)}, f32[3,10,1,128]{3,2,1,0:T(1,128)S(1)}, u32[]{:S(2)}, u32[]{:S(2)}) collective-permute-start(f32[3,10,1,128]{3,2,1,0:T(1,128)S(1)} %get-tuple-element.22), channel_id=1, source_target_pairs={{0,1},{1,2},{2,3},{3,4},{4,5},{5,6},{6,7},{7,0},{8,9},{9,10},{10,1... | collective-permute-start | bytes 46088 | tf_op jit(solution)/shard_map/ppermute | solution.py:16
